TPU v7x, 32 devices: a whole 2x2x4 slice. The times are simulated.
32 devices in a mesh: groups: 2 (over y), patch: 4 (over z), sub: 2 (over x), half: 2 (over core).
Axes of the slice: x: 2, y: 2, z: 4, core: 2. Of those that a mesh axis runs over, the one named last changes fastest.
Arguments:
- vectors: float32 [2, 8192, 256], P(None, ('groups', 'patch', 'sub', 'half')), parts along dimension 1, may hold values from -600 to 600
- prestress: bfloat16 [8192, 3, 256], P(('groups', 'patch', 'sub', 'half')), parts along dimension 0, may hold values from -4 to 4
- thickness: float32 [8192, 256], P(('groups', 'patch', 'sub', 'half')), parts along dimension 0, may hold values from 0.5 to 2
- foundation: float32 [8192, 256], P(('groups', 'patch', 'sub', 'half')), parts along dimension 0, may hold values from 2 to 6
- patch_rows: int32 [64], P(('groups', 'patch', 'sub', 'half')), parts along dimension 0, may hold values from 64 to 128, as said below
- matched: int32 [64], P(('groups', 'patch', 'sub', 'half')), parts along dimension 0, may hold values from 0 to 31, as said below
- elem_row: int32 [8192], P(('groups', 'patch', 'sub', 'half')), parts along dimension 0, may hold values from 0 to 4095, as said below
Outputs:
- modes: float32 [2, 8192, 256], P(None, ('groups', 'patch', 'sub', 'half')), parts along dimension 1
There are 2 independent parts, one for each index of `groups`. A program takes and returns all parts, laid end to end along the dimension named above; each array names one. Nothing has to cross between parts.
Inputs may be any that keep to these rules, and one draw needn't show every extreme that they name: `patch_rows`: the largest value is reached by some patch in every draw. A permutation of the patches; the patch matched to a patch lies on the device with the same sub and half indices and a patch index one above or one below, cyclically. `elem_row`: a permutation of the rows; of each device's rows, those in positions k * 16 to (k + 1) * 16 - 1 belong to patches of the device with index k along patch+sub+half.
All inputs are finite; a program needn't handle non-finite values.
Results may differ from a plain program's by a relative error of at most 0.0003.
Values may be sent and summed in bfloat16 or wider, within the bound.
A program may use at most 64 MiB of HBM per device.

v0:
```python
import jax
import jax.numpy as jnp
from jax import lax
from jax.sharding import PartitionSpec as P

ITERS = 2
step_size = 1.0
norm_scale = 16.0
penalty_value = 8.0
penalty_slope = 4.0


def passed_along(array, axis, by):
    peers = lax.axis_size(axis)
    return lax.ppermute(array, axis, [(i, (i + by) % peers) for i in range(peers)])


def second_rows(field):
    padded = jnp.pad(field, [(0, 0)] * (field.ndim - 2) + [(1, 1), (0, 0)])
    return padded[..., :-2, :] - 2.0 * field + padded[..., 2:, :]


def second_cols(field):
    padded = jnp.pad(field, [(0, 0)] * (field.ndim - 1) + [(1, 1)])
    return padded[..., :-2] - 2.0 * field + padded[..., 2:]


def forward_rows(field):
    zeros = jnp.zeros_like(field[..., :1, :])
    return jnp.concatenate([field[..., 1:, :], zeros], axis=-2) - field


def backward_rows(field):
    zeros = jnp.zeros_like(field[..., :1, :])
    return jnp.concatenate([zeros, field[..., :-1, :]], axis=-2) - field


def forward_cols(field):
    zeros = jnp.zeros_like(field[..., :1])
    return jnp.concatenate([field[..., 1:], zeros], axis=-1) - field


def backward_cols(field):
    zeros = jnp.zeros_like(field[..., :1])
    return jnp.concatenate([zeros, field[..., :-1]], axis=-1) - field


def stiffness(field, live, thickness, foundation):
    bend_rows = thickness * live * second_rows(field)
    bend_cols = thickness * second_cols(field)
    return live * (foundation * field + second_rows(bend_rows) + second_cols(bend_cols))


def geometric(field, live, stress):
    along_rows = forward_rows(field)
    along_cols = forward_cols(field)
    nuu = stress[:, :, 0, :]
    nvv = stress[:, :, 1, :]
    nuv = stress[:, :, 2, :]
    total = backward_rows(nuu * along_rows + nuv * along_cols) + backward_cols(
        nvv * along_cols + nuv * along_rows
    )
    return live * total


def edges(field, lengths):

    def row_pick(index):
        where_rows = jnp.broadcast_to(
            index[None, :, None, None], (field.shape[0], field.shape[1], 1, field.shape[3])
        )
        return jnp.take_along_axis(field, where_rows, axis=2)[:, :, 0, :]

    top = jnp.stack([row_pick(lengths - 2), row_pick(lengths - 1)], axis=2)
    bottom = field[:, :, 0:2, :]
    return (top, bottom)


def interface(field, lengths, top, bottom, partner_top, partner_bottom):
    jump_top = top[:, :, 1, :] - partner_bottom[:, :, 0, :]
    slope_top = (
        top[:, :, 1, :]
        - top[:, :, 0, :]
        - (partner_bottom[:, :, 1, :] - partner_bottom[:, :, 0, :])
    )
    jump_bottom = partner_top[:, :, 1, :] - bottom[:, :, 0, :]
    slope_bottom = (
        partner_top[:, :, 1, :]
        - partner_top[:, :, 0, :]
        - (bottom[:, :, 1, :] - bottom[:, :, 0, :])
    )
    rows = jnp.arange(field.shape[2], dtype=jnp.int32)[None, :, None]
    last = lengths[:, None, None] - 1
    added = jnp.where(
        rows == last, (penalty_value * jump_top + penalty_slope * slope_top)[:, :, None, :], 0.0
    )
    added = added + jnp.where(rows == last - 1, (-penalty_slope * slope_top)[:, :, None, :], 0.0)
    added = added + jnp.where(
        rows == 0, (-penalty_value * jump_bottom + penalty_slope * slope_bottom)[:, :, None, :], 0.0
    )
    added = added + jnp.where(rows == 1, (-penalty_slope * slope_bottom)[:, :, None, :], 0.0)
    return added


def products(field, kfield, gfield):
    return jnp.stack(
        [
            jnp.sum(field[0] * kfield[0]),
            jnp.sum(field[0] * kfield[1]),
            jnp.sum(field[1] * kfield[1]),
            jnp.sum(field[0] * gfield[0]),
            jnp.sum(field[0] * gfield[1]),
            jnp.sum(field[1] * gfield[1]),
        ]
    )


def advance(field, kfield, gfield, totals, precond, cells):
    first_a = totals[0]
    cross_k = totals[1]
    second_a = totals[2]
    first_g = totals[3]
    cross_g = totals[4]
    second_g = totals[5]
    ratio = cross_k / first_a
    other = field[1] - ratio * field[0]
    other_k = kfield[1] - ratio * kfield[0]
    other_g = gfield[1] - ratio * gfield[0]
    other_a = second_a - ratio * cross_k
    other_q = second_g - 2.0 * ratio * cross_g + ratio * ratio * first_g
    first_mu = first_g / first_a
    other_mu = other_q / other_a
    new_first = (field[0] + step_size * precond * (gfield[0] - first_mu * kfield[0])) * jnp.sqrt(
        norm_scale * cells / first_a
    )
    new_other = (other + step_size * precond * (other_g - other_mu * other_k)) * jnp.sqrt(
        norm_scale * cells / other_a
    )
    return jnp.stack([new_first, new_other])


def choose(candidates, wanted, labels):
    match = labels[None, :] == wanted[:, None]
    return jnp.sum(jnp.where(match[None, :, :, None, None], candidates[:, None], 0.0), axis=2)


def per_device(vectors, prestress, thickness, foundation, patch_rows, matched, elem_row):
    owners = lax.axis_size("patch")
    inner = lax.axis_size(("sub", "half"))
    slots = patch_rows.shape[0]
    rows_dev = thickness.shape[0]
    prows = rows_dev // slots
    ncol = thickness.shape[1]
    per_peer = rows_dev // (owners * inner)
    blocks = prestress.reshape(owners, inner, per_peer, 3, ncol)
    targets = (elem_row % rows_dev).reshape(owners, inner, per_peer)
    arrived, arrived_rows = (
        lax.all_to_all(
            lax.all_to_all(blocks, "patch", split_axis=0, concat_axis=0, tiled=True),
            ("sub", "half"),
            split_axis=1,
            concat_axis=1,
            tiled=True,
        ),
        lax.all_to_all(
            lax.all_to_all(targets, "patch", split_axis=0, concat_axis=0, tiled=True),
            ("sub", "half"),
            split_axis=1,
            concat_axis=1,
            tiled=True,
        ),
    )
    placed = (
        jnp.zeros((rows_dev, 3, ncol), jnp.bfloat16)
        .at[arrived_rows.reshape(-1)]
        .set(arrived.reshape(-1, 3, ncol))
    )
    stress = placed.astype(jnp.float32).reshape(slots, prows, 3, ncol)
    rows = jnp.arange(prows, dtype=jnp.int32)[None, :]
    live = (rows < patch_rows[:, None]).astype(jnp.float32)[:, :, None]
    thick = thickness.reshape(slots, prows, ncol)
    support = foundation.reshape(slots, prows, ncol)
    precond = live / (support + 12.0 * thick)
    own_ids = lax.axis_index(("patch", "sub", "half")) * slots + jnp.arange(slots, dtype=jnp.int32)
    labels = jnp.stack([own_ids, matched])
    field = vectors.reshape(2, slots, prows, ncol) * live
    cells = jnp.float32(owners * inner * rows_dev * ncol)
    for step in range(ITERS):
        top, bottom = edges(field, patch_rows)
        strips = jnp.stack([top, bottom])
        below = passed_along((strips, labels), "patch", 1)
        above = passed_along((strips, labels), "patch", -1)
        got_strips = jnp.stack([below[0], above[0]])
        got_labels = jnp.stack([below[1], above[1]])
        count = got_strips.shape[0] * slots
        cand_top = jnp.moveaxis(got_strips[:, 0], 0, 1).reshape(2, count, 2, ncol)
        cand_bottom = jnp.moveaxis(got_strips[:, 1], 0, 1).reshape(2, count, 2, ncol)
        cand_ids = got_labels[:, 0].reshape(-1)
        cand_next = got_labels[:, 1].reshape(-1)
        partner_bottom = choose(cand_bottom, matched, cand_ids)
        partner_top = choose(cand_top, own_ids, cand_next)
        kfield = stiffness(field, live, thick, support) + interface(
            field, patch_rows, top, bottom, partner_top, partner_bottom
        )
        gfield = geometric(field, live, stress)
        totals = lax.psum(products(field, kfield, gfield), ("patch", "sub", "half"))
        field = advance(field, kfield, gfield, totals, precond, cells)
    return field.reshape(2, rows_dev, ncol)


def solution(mesh):
    in_specs = (
        P(None, ("groups", "patch", "sub", "half"), None),
        P(("groups", "patch", "sub", "half"), None, None),
        P(("groups", "patch", "sub", "half"), None),
        P(("groups", "patch", "sub", "half"), None),
        P(("groups", "patch", "sub", "half")),
        P(("groups", "patch", "sub", "half")),
        P(("groups", "patch", "sub", "half")),
    )
    out_specs = P(None, ("groups", "patch", "sub", "half"), None)
    return jax.shard_map(
        per_device, mesh=mesh, in_specs=in_specs, out_specs=out_specs, check_vma=False
    )
```

profile of v0, /device:TPU:0, one launch (start us, length us, event | category | flops | bytes accessed | tf_op | source)
XLA Modules:
  0.0 211.1 jit_solution(15988298672852159609)
XLA Ops:
  0.0 0.7 broadcast_add_fusion
  1.1 1.1 broadcast_multiply_fusion
  2.2 12.3 %gather_fusion = f32[1024]{0:T(1024)S(1)} fusion(f32[2,2,128,256]{3,2,1,0:T(8,128)S(1)} %broadcast_multiply_fusion, s32[1024]{0:T(1024)S(1)} %bitcast.210), kind=kCustom, calls=%fused_computation.clone | custom fusion | bytes 24576 | tf_op jit(solution)/shard_map/jit(take_along_axis)/gather | solution.py:72
  14.6 12.3 %gather_fusion.1 = f32[1024]{0:T(1024)S(1)} fusion(f32[2,2,128,256]{3,2,1,0:T(8,128)S(1)} %broadcast_multiply_fusion, s32[1024]{0:T(1024)S(1)} %bitcast.212), kind=kCustom, calls=%fused_computation.1.clone | custom fusion | bytes 24576 | tf_op jit(solution)/shard_map/jit(take_along_axis)/gather | solution.py:72
  27.1 3.1 %collective-permute-start.2 = (f32[2,2,2,2,256]{4,3,2,1,0:T(2,128)S(1)}, f32[2,2,2,2,256]{4,3,2,1,0:T(2,128)S(1)}, u32[]{:S(2)}, u32[]{:S(2)}) collective-permute-start(f32[2,2,2,2,256]{4,3,2,1,0:T(2,128)S(1)} %pad_maximum_fusion.4), channel_id=1, source_target_pairs={{0,4},{4,8},{8,12},{12,0},{1,5},{5,9},{9,13},{13,1},{2,6},{6,10},{... | collective-permute-start | bytes 49160 | tf_op jit(solution)/shard_map/ppermute | solution.py:15
  30.1 2.1 collective-permute-start.3
  32.2 0.7 copy-done.13
  33.0 3.8 %collective-permute-start.1 = (s32[2,2]{1,0:T(2,128)S(1)}, s32[2,2]{1,0:T(2,128)S(1)}, u32[]{:S(2)}, u32[]{:S(2)}) collective-permute-start(s32[2,2]{1,0:T(2,128)S(1)} %pad_add_fusion.4), channel_id=1, source_target_pairs={{0,12},{4,0},{8,4},{12,8},{1,13},{5,1},{9,5},{13,9},{2,14},{6,2},{... | collective-permute-start | bytes 56 | tf_op jit(solution)/shard_map/ppermute | solution.py:15
  36.8 0.7 reshape.291
  37.5 3.2 %all-to-all-start = ((s32[4,4,16]{2,1,0:T(4,128)}), s32[4,4,16]{2,1,0:T(4,128)S(1)}, u32[]{:S(2)}, u32[]{:S(2)}) async-start(s32[4,4,16]{2,1,0:T(4,128)} %reshape.291), calls=%async_computation | async-start | bytes 16384 | tf_op jit(solution)/shard_map/all_to_all | solution.py:166
  40.8 1.0 slice.350
  42.0 0.8 copy-done.10
  42.8 0.8 copy.30
  43.8 2.4 %all-to-all-done = s32[4,4,16]{2,1,0:T(4,128)S(1)} async-done(((s32[4,4,16]{2,1,0:T(4,128)}), s32[4,4,16]{2,1,0:T(4,128)S(1)}, u32[]{:S(2)}, u32[]{:S(2)}) %all-to-all-start) | async-done | bytes 1056 | tf_op jit(solution)/shard_map/all_to_all | solution.py:166
  46.3 0.6 copy.28
  46.9 3.2 %all-to-all-start.1 = ((s32[4,4,16]{2,0,1:T(4,128)}), s32[4,4,16]{2,0,1:T(4,128)S(1)}, u32[]{:S(2)}, u32[]{:S(2)}) async-start(s32[4,4,16]{2,0,1:T(4,128)} %copy.28), calls=%async_computation.1 | async-start | bytes 16384 | tf_op jit(solution)/shard_map/all_to_all | solution.py:165
  50.2 3.7 %all-to-all-done.1 = s32[4,4,16]{2,0,1:T(4,128)S(1)} async-done(((s32[4,4,16]{2,0,1:T(4,128)}), s32[4,4,16]{2,0,1:T(4,128)S(1)}, u32[]{:S(2)}, u32[]{:S(2)}) %all-to-all-start.1) | async-done | bytes 1056 | tf_op jit(solution)/shard_map/all_to_all | solution.py:165
  53.9 3.5 %all-to-all-start.2 = ((bf16[4,4,16,3,256]{4,2,1,3,0:T(8,128)(2,1)}), bf16[4,4,16,3,256]{4,2,1,3,0:T(8,128)(2,1)S(1)}, u32[]{:S(2)}, u32[]{:S(2)}) async-start(bf16[4,4,16,3,256]{4,2,1,3,0:T(8,128)(2,1)} %copy.30), calls=%async_computation.2 | async-start | bytes 786432 | tf_op jit(solution)/shard_map/all_to_all | solution.py:159
  57.8 11.4 %all-to-all-done.2 = bf16[4,4,16,3,256]{4,2,1,3,0:T(8,128)(2,1)S(1)} async-done(((bf16[4,4,16,3,256]{4,2,1,3,0:T(8,128)(2,1)}), bf16[4,4,16,3,256]{4,2,1,3,0:T(8,128)(2,1)S(1)}, u32[]{:S(2)}, u32[]{:S(2)}) %all-to-all-start.2) | async-done | bytes 393248 | tf_op jit(solution)/shard_map/all_to_all | solution.py:159
  69.2 0.8 copy.31
  70.0 3.5 %all-to-all-start.3 = ((bf16[4,4,16,3,256]{4,2,0,3,1:T(8,128)(2,1)}), bf16[4,4,16,3,256]{4,2,0,3,1:T(8,128)(2,1)S(1)}, u32[]{:S(2)}, u32[]{:S(2)}) async-start(bf16[4,4,16,3,256]{4,2,0,3,1:T(8,128)(2,1)} %copy.31), calls=%async_computation.3 | async-start | bytes 786432 | tf_op jit(solution)/shard_map/all_to_all | solution.py:158
  73.6 7.3 %all-to-all-done.3 = bf16[4,4,16,3,256]{4,2,0,3,1:T(8,128)(2,1)S(1)} async-done(((bf16[4,4,16,3,256]{4,2,0,3,1:T(8,128)(2,1)}), bf16[4,4,16,3,256]{4,2,0,3,1:T(8,128)(2,1)S(1)}, u32[]{:S(2)}, u32[]{:S(2)}) %all-to-all-start.3) | async-done | bytes 393248 | tf_op jit(solution)/shard_map/all_to_all | solution.py:158
  80.9 0.3 copy.33
  81.4 7.0 %scatter_fusion = bf16[256,3,256]{2,1,0:T(4,128)(2,1)S(1)} fusion(bf16[256,3,256]{2,1,0:T(4,128)(2,1)S(1)} %broadcast_in_dim.225, s32[256]{0:T(256)S(1)} %bitcast.260, bf16[256,3,256]{2,1,0:T(4,128)(2,1)S(1)} %copy.33), kind=kCustom, calls=%fused_computation.4 | custom fusion | bytes 1180672 | tf_op jit(solution)/shard_map/scatter | solution.py:176
  88.4 0.5 fusion.89
  89.1 1.2 copy-done.7
  90.2 0.5 fusion.20
  90.7 0.5 copy-done.1
  91.3 0.8 fusion.8
  92.2 0.8 fusion.37
  93.0 3.8 %stack.135 = f32[6]{0:T(128)S(1)} concatenate(f32[1]{0:T(128)} %bitcast.30, f32[1]{0:T(128)} %bitcast.32, f32[1]{0:T(128)} %bitcast.34, f32[1]{0:T(128)} %bitcast.36, f32[1]{0:T(128)} %bitcast.38, f32[1]{0:T(128)} %bitcast.39), dimensions={0} | concatenate | bytes 48 | tf_op jit(solution)/shard_map/stack | solution.py:106
  96.8 30.2 %psum.14 = f32[6]{0:T(128)S(1)} all-reduce(f32[6]{0:T(128)S(1)} %stack.135), channel_id=1, replica_groups=mesh['groups'=2,'patch'=4,'sub'=2,'half'=2] {'patch','sub','half'}, use_global_device_ids=true, to_apply=%region_9.11 | all-reduce | flops 6 | bytes 48 | tf_op jit(solution)/shard_map/psum | solution.py:206
  127.1 0.7 fusion.91
  134.1 1.0 fusion.41
  135.6 0.9 copy-done.3
  136.7 12.3 %gather_fusion.3 = f32[1024]{0:T(1024)S(1)} fusion(f32[2,2,128,256]{3,2,1,0:T(8,128)S(1)} %get-tuple-element.46, s32[1024]{0:T(1024)S(1)} %bitcast.213), kind=kCustom, calls=%fused_computation.3.clone | custom fusion | bytes 24576 | tf_op jit(solution)/shard_map/jit(take_along_axis)/gather | solution.py:72
  149.1 12.3 %gather_fusion.2 = f32[1024]{0:T(1024)S(1)} fusion(f32[2,2,128,256]{3,2,1,0:T(8,128)S(1)} %get-tuple-element.46, s32[1024]{0:T(1024)S(1)} %bitcast.211), kind=kCustom, calls=%fused_computation.2.clone | custom fusion | bytes 24576 | tf_op jit(solution)/shard_map/jit(take_along_axis)/gather | solution.py:72
  161.6 3.8 %collective-permute-start.5 = (f32[2,2,2,2,256]{4,3,2,1,0:T(2,128)S(1)}, f32[2,2,2,2,256]{4,3,2,1,0:T(2,128)S(1)}, u32[]{:S(2)}, u32[]{:S(2)}) collective-permute-start(f32[2,2,2,2,256]{4,3,2,1,0:T(2,128)S(1)} %pad_maximum_fusion.5), channel_id=1, source_target_pairs={{0,12},{4,0},{8,4},{12,8},{1,13},{5,1},{9,5},{13,9},{2,14},{6,2},{... | collective-permute-start | bytes 49160 | tf_op jit(solution)/shard_map/ppermute | solution.py:15
  165.5 0.4 fusion.25
  165.8 0.2 add_multiply_fusion
  166.1 1.1 collective-permute-done.4
  167.7 0.6 fusion.17
  168.3 0.3 copy-done.8
  168.7 0.8 fusion.33
  169.5 3.8 %stack.150 = f32[6]{0:T(128)S(1)} concatenate(f32[1]{0:T(128)} %bitcast.59, f32[1]{0:T(128)} %bitcast.61, f32[1]{0:T(128)} %bitcast.62, f32[1]{0:T(128)} %bitcast.64, f32[1]{0:T(128)} %bitcast.66, f32[1]{0:T(128)} %bitcast.67), dimensions={0} | concatenate | bytes 48 | tf_op jit(solution)/shard_map/stack | solution.py:106
  173.4 29.5 %psum.15 = f32[6]{0:T(128)S(1)} all-reduce(f32[6]{0:T(128)S(1)} %stack.150), channel_id=1, replica_groups=mesh['groups'=2,'patch'=4,'sub'=2,'half'=2] {'patch','sub','half'}, use_global_device_ids=true, to_apply=%region_18.20 | all-reduce | flops 6 | bytes 48 | tf_op jit(solution)/shard_map/psum | solution.py:206
  202.9 0.7 fusion.90
  210.3 0.8 pad_maximum_fusion.1
  (106 shorter events, 3.6 us)
Async XLA Ops:
  0.0 0.7 copy-start.12
  27.1 30.4 %collective-permute-start.2 = (f32[2,2,2,2,256]{4,3,2,1,0:T(2,128)S(1)}, f32[2,2,2,2,256]{4,3,2,1,0:T(2,128)S(1)}, u32[]{:S(2)}, u32[]{:S(2)}) collective-permute-start(f32[2,2,2,2,256]{4,3,2,1,0:T(2,128)S(1)} %pad_maximum_fusion.4), channel_id=1, source_target_pairs={{0,4},{4,8},{8,12},{12,0},{1,5},{5,9},{9,13},{13,1},{2,6},{6,10},{... | collective-permute-start | bytes 49160 | tf_op jit(solution)/shard_map/ppermute | solution.py:15
  30.1 27.3 %collective-permute-start.3 = (f32[2,2,2,2,256]{4,3,2,1,0:T(2,128)S(1)}, f32[2,2,2,2,256]{4,3,2,1,0:T(2,128)S(1)}, u32[]{:S(2)}, u32[]{:S(2)}) collective-permute-start(f32[2,2,2,2,256]{4,3,2,1,0:T(2,128)S(1)} %pad_maximum_fusion.4), channel_id=1, source_target_pairs={{0,12},{4,0},{8,4},{12,8},{1,13},{5,1},{9,5},{13,9},{2,14},{6,2},{... | collective-permute-start | bytes 49160 | tf_op jit(solution)/shard_map/ppermute | solution.py:15
  32.2 0.7 copy-start.13
  32.9 3.9 %copy-start.11 = (s32[256]{0:T(256)S(1)}, s32[256]{0:T(256)}, u32[]{:S(2)}) copy-start(s32[256]{0:T(256)} %param.15) | copy-start | bytes 3076
  32.9 10.7 %collective-permute-start = (s32[2,2]{1,0:T(2,128)S(1)}, s32[2,2]{1,0:T(2,128)S(1)}, u32[]{:S(2)}, u32[]{:S(2)}) collective-permute-start(s32[2,2]{1,0:T(2,128)S(1)} %pad_add_fusion.4), channel_id=1, source_target_pairs={{0,4},{4,8},{8,12},{12,0},{1,5},{5,9},{9,13},{13,1},{2,6},{6,10},{... | collective-permute-start | bytes 56 | tf_op jit(solution)/shard_map/ppermute | solution.py:15
  33.0 10.6 %collective-permute-start.1 = (s32[2,2]{1,0:T(2,128)S(1)}, s32[2,2]{1,0:T(2,128)S(1)}, u32[]{:S(2)}, u32[]{:S(2)}) collective-permute-start(s32[2,2]{1,0:T(2,128)S(1)} %pad_add_fusion.4), channel_id=1, source_target_pairs={{0,12},{4,0},{8,4},{12,8},{1,13},{5,1},{9,5},{13,9},{2,14},{6,2},{... | collective-permute-start | bytes 56 | tf_op jit(solution)/shard_map/ppermute | solution.py:15
  37.5 8.8 %all-to-all-start = ((s32[4,4,16]{2,1,0:T(4,128)}), s32[4,4,16]{2,1,0:T(4,128)S(1)}, u32[]{:S(2)}, u32[]{:S(2)}) async-start(s32[4,4,16]{2,1,0:T(4,128)} %reshape.291), calls=%async_computation | async-start | bytes 16384 | tf_op jit(solution)/shard_map/all_to_all | solution.py:166
  40.8 1.1 copy-start
  41.8 1.0 copy-start.10
  46.9 7.0 %all-to-all-start.1 = ((s32[4,4,16]{2,0,1:T(4,128)}), s32[4,4,16]{2,0,1:T(4,128)S(1)}, u32[]{:S(2)}, u32[]{:S(2)}) async-start(s32[4,4,16]{2,0,1:T(4,128)} %copy.28), calls=%async_computation.1 | async-start | bytes 16384 | tf_op jit(solution)/shard_map/all_to_all | solution.py:165
  53.9 15.4 %all-to-all-start.2 = ((bf16[4,4,16,3,256]{4,2,1,3,0:T(8,128)(2,1)}), bf16[4,4,16,3,256]{4,2,1,3,0:T(8,128)(2,1)S(1)}, u32[]{:S(2)}, u32[]{:S(2)}) async-start(bf16[4,4,16,3,256]{4,2,1,3,0:T(8,128)(2,1)} %copy.30), calls=%async_computation.2 | async-start | bytes 786432 | tf_op jit(solution)/shard_map/all_to_all | solution.py:159
  70.0 10.9 %all-to-all-start.3 = ((bf16[4,4,16,3,256]{4,2,0,3,1:T(8,128)(2,1)}), bf16[4,4,16,3,256]{4,2,0,3,1:T(8,128)(2,1)S(1)}, u32[]{:S(2)}, u32[]{:S(2)}) async-start(bf16[4,4,16,3,256]{4,2,0,3,1:T(8,128)(2,1)} %copy.31), calls=%async_computation.3 | async-start | bytes 786432 | tf_op jit(solution)/shard_map/all_to_all | solution.py:158
  89.0 1.2 copy-start.7
  89.0 1.6 copy-start.2
  89.0 1.6 copy-start.4
  90.2 0.9 copy-start.1
  90.2 1.1 copy-start.6
  135.5 1.0 copy-start.3
  135.5 1.0 copy-start.5
  161.6 5.6 %collective-permute-start.4 = (f32[2,2,2,2,256]{4,3,2,1,0:T(2,128)S(1)}, f32[2,2,2,2,256]{4,3,2,1,0:T(2,128)S(1)}, u32[]{:S(2)}, u32[]{:S(2)}) collective-permute-start(f32[2,2,2,2,256]{4,3,2,1,0:T(2,128)S(1)} %pad_maximum_fusion.5), channel_id=1, source_target_pairs={{0,4},{4,8},{8,12},{12,0},{1,5},{5,9},{9,13},{13,1},{2,6},{6,10},{... | collective-permute-start | bytes 49160 | tf_op jit(solution)/shard_map/ppermute | solution.py:15
  161.6 5.5 %collective-permute-start.5 = (f32[2,2,2,2,256]{4,3,2,1,0:T(2,128)S(1)}, f32[2,2,2,2,256]{4,3,2,1,0:T(2,128)S(1)}, u32[]{:S(2)}, u32[]{:S(2)}) collective-permute-start(f32[2,2,2,2,256]{4,3,2,1,0:T(2,128)S(1)} %pad_maximum_fusion.5), channel_id=1, source_target_pairs={{0,12},{4,0},{8,4},{12,8},{1,13},{5,1},{9,5},{13,9},{2,14},{6,2},{... | collective-permute-start | bytes 49160 | tf_op jit(solution)/shard_map/ppermute | solution.py:15
  167.6 1.0 copy-start.8
  167.7 1.0 copy-start.9
where the time goes:
time: 212 us; the launch traced here: 211 us
  local copies, waits for them, and re-layouts  75.2 us (35%)
  blocking collectives  59.7 us (28%)
  starting transfers between devices  26.3 us (12%)
  waiting for transfers between devices  26 us (12%)
  between operations  13.6 us (6%)
  other arithmetic  10.3 us (5%)
    psum x2, blocking collectives, per_device(): totals = lax.psum(products(field, kfield, gfield), ('patch', 'sub', 'half'))  59.7 us
    gather x4, local copies, waits for them, and re-layouts, row_pick(): return jnp.take_along_axis(field, where_rows, axis=2)[:, :, 0, :]  49.2 us
    ppermute x6, starting transfers between devices, passed_along(): lax.ppermute(array, axis, [(i, (i + by) % peers) for i in range(peers)])  12.9 us
    all_to_all x1, waiting for transfers between devices, per_device(): lax.all_to_all(blocks, 'patch', split_axis=0, concat_axis=0, tiled=True)  11.4 us
    another operation x2, local copies, waits for them, and re-layouts, products(): jnp.stack([jnp.sum(field[0] * kfield[0]), jnp.sum(field[0] * kfield[1]),...  7.63 us
    all_to_all x1, waiting for transfers between devices, per_device(): lax.all_to_all(lax.all_to_all(blocks, 'patch', split_axis=0, concat_axis=...  7.33 us
    scatter x1, local copies, waits for them, and re-layouts, per_device(): placed = jnp.zeros((rows_dev, 3, ncol), jnp.bfloat16).at[arrived_rows.res...  6.97 us
    unnamed x40, local copies, waits for them, and re-layouts  4.77 us
  transfers between devices with their start and end apart: 10, of which 5 were waited for; matrix products, arithmetic and copies ran while one was open for 2% of the time, Pallas kernels for 0%

commit v1 on v0

--- a/solution.py
+++ b/solution.py
@@ -203,7 +203,9 @@
             field, patch_rows, top, bottom, partner_top, partner_bottom
         )
         gfield = geometric(field, live, stress)
-        totals = lax.psum(products(field, kfield, gfield), ("patch", "sub", "half"))
+        x = products(field, kfield, gfield)
+        pieces = lax.all_gather(x, ("patch", "sub", "half"))
+        totals = jnp.sum(pieces, axis=0)
         field = advance(field, kfield, gfield, totals, precond, cells)
     return field.reshape(2, rows_dev, ncol)
 

time: 212 us -> 214 us (level)
  waiting for transfers between devices: 26 us -> 23.6 us
    psum x2 -> x0, blocking collectives: 59.7 us -> none  [per_device(): totals = lax.psum(products(field, kfield, gfield), ('patch', 'sub', 'half'))]
    unnamed x0 -> x2, blocking collectives: none -> 59.7 us
    all_to_all x1, waiting for transfers between devices: 2.45 us -> 0.25 us  [per_device(): lax.all_to_all(targets, 'patch', split_axis=0, concat_axis=0, tiled=True)]
    unnamed x40 -> x47, local copies, waits for them, and re-layouts: 4.77 us -> 6.62 us
  transfers between devices with their start and end apart: 10 -> 10, of which waited for: 5 -> 5; matrix products, arithmetic and copies ran while one was open for 2% -> 3% of each run, Pallas kernels for 0% -> 0%
where the time goes in v1:
time: 214 us; the launch traced here: 213 us
  local copies, waits for them, and re-layouts  77.2 us (36%)
  blocking collectives  59.7 us (28%)
  starting transfers between devices  27.6 us (13%)
  waiting for transfers between devices  23.6 us (11%)
  between operations  14.2 us (7%)
  other arithmetic  10.4 us (5%)
    unnamed x2, blocking collectives  59.7 us
    gather x4, local copies, waits for them, and re-layouts, row_pick(): return jnp.take_along_axis(field, where_rows, axis=2)[:, :, 0, :]  49.2 us
    ppermute x6, starting transfers between devices, passed_along(): lax.ppermute(array, axis, [(i, (i + by) % peers) for i in range(peers)])  12.9 us
    all_to_all x1, waiting for transfers between devices, per_device(): lax.all_to_all(blocks, 'patch', split_axis=0, concat_axis=0, tiled=True)  11.2 us
    another operation x2, local copies, waits for them, and re-layouts, products(): jnp.stack([jnp.sum(field[0] * kfield[0]), jnp.sum(field[0] * kfield[1]),...  7.63 us
    all_to_all x1, waiting for transfers between devices, per_device(): lax.all_to_all(lax.all_to_all(blocks, 'patch', split_axis=0, concat_axis=...  7.33 us
    scatter x1, local copies, waits for them, and re-layouts, per_device(): placed = jnp.zeros((rows_dev, 3, ncol), jnp.bfloat16).at[arrived_rows.res...  6.97 us
    unnamed x47, local copies, waits for them, and re-layouts  6.62 us
  transfers between devices with their start and end apart: 10, of which 5 were waited for; matrix products, arithmetic and copies ran while one was open for 3% of the time, Pallas kernels for 0%

profile of v1, /device:TPU:0, one launch (start us, length us, event | category | flops | bytes accessed | tf_op | source)
XLA Modules:
  0.0 212.7 jit_solution(16230711869968738362)
XLA Ops:
  0.0 0.7 broadcast_add_fusion
  1.1 1.1 broadcast_multiply_fusion
  2.2 12.3 %gather_fusion = f32[1024]{0:T(1024)S(1)} fusion(f32[2,2,128,256]{3,2,1,0:T(8,128)S(1)} %broadcast_multiply_fusion, s32[1024]{0:T(1024)S(1)} %bitcast.211), kind=kCustom, calls=%fused_computation.clone | custom fusion | bytes 24576 | tf_op jit(solution)/shard_map/jit(take_along_axis)/gather | solution.py:72
  14.6 12.3 %gather_fusion.1 = f32[1024]{0:T(1024)S(1)} fusion(f32[2,2,128,256]{3,2,1,0:T(8,128)S(1)} %broadcast_multiply_fusion, s32[1024]{0:T(1024)S(1)} %bitcast.213), kind=kCustom, calls=%fused_computation.1.clone | custom fusion | bytes 24576 | tf_op jit(solution)/shard_map/jit(take_along_axis)/gather | solution.py:72
  27.1 3.1 %collective-permute-start.2 = (f32[2,2,2,2,256]{4,3,2,1,0:T(2,128)S(1)}, f32[2,2,2,2,256]{4,3,2,1,0:T(2,128)S(1)}, u32[]{:S(2)}, u32[]{:S(2)}) collective-permute-start(f32[2,2,2,2,256]{4,3,2,1,0:T(2,128)S(1)} %pad_maximum_fusion.4), channel_id=1, source_target_pairs={{0,4},{4,8},{8,12},{12,0},{1,5},{5,9},{9,13},{13,1},{2,6},{6,10},{... | collective-permute-start | bytes 49160 | tf_op jit(solution)/shard_map/ppermute | solution.py:15
  30.1 2.1 collective-permute-start.3
  32.2 0.7 copy-done.13
  33.0 3.8 %collective-permute-start.1 = (s32[2,2]{1,0:T(2,128)S(1)}, s32[2,2]{1,0:T(2,128)S(1)}, u32[]{:S(2)}, u32[]{:S(2)}) collective-permute-start(s32[2,2]{1,0:T(2,128)S(1)} %pad_add_fusion.4), channel_id=1, source_target_pairs={{0,12},{4,0},{8,4},{12,8},{1,13},{5,1},{9,5},{13,9},{2,14},{6,2},{... | collective-permute-start | bytes 56 | tf_op jit(solution)/shard_map/ppermute | solution.py:15
  36.8 0.7 reshape.291
  37.5 3.2 %all-to-all-start = ((s32[4,4,16]{2,1,0:T(4,128)}), s32[4,4,16]{2,1,0:T(4,128)S(1)}, u32[]{:S(2)}, u32[]{:S(2)}) async-start(s32[4,4,16]{2,1,0:T(4,128)} %reshape.291), calls=%async_computation | async-start | bytes 16384 | tf_op jit(solution)/shard_map/all_to_all | solution.py:166
  40.8 1.0 slice.350
  42.0 0.8 copy-done.10
  42.8 0.8 copy.30
  43.8 0.6 copy-done.14
  44.5 0.6 dynamic-slice
  46.3 0.6 copy.28
  46.9 3.2 %all-to-all-start.1 = ((s32[4,4,16]{2,0,1:T(4,128)}), s32[4,4,16]{2,0,1:T(4,128)S(1)}, u32[]{:S(2)}, u32[]{:S(2)}) async-start(s32[4,4,16]{2,0,1:T(4,128)} %copy.28), calls=%async_computation.1 | async-start | bytes 16384 | tf_op jit(solution)/shard_map/all_to_all | solution.py:165
  50.2 3.7 %all-to-all-done.1 = s32[4,4,16]{2,0,1:T(4,128)S(1)} async-done(((s32[4,4,16]{2,0,1:T(4,128)}), s32[4,4,16]{2,0,1:T(4,128)S(1)}, u32[]{:S(2)}, u32[]{:S(2)}) %all-to-all-start.1) | async-done | bytes 1056 | tf_op jit(solution)/shard_map/all_to_all | solution.py:165
  53.9 4.8 %all-to-all-start.2 = ((bf16[4,4,16,3,256]{4,2,1,3,0:T(8,128)(2,1)}), bf16[4,4,16,3,256]{4,2,1,3,0:T(8,128)(2,1)S(1)}, u32[]{:S(2)}, u32[]{:S(2)}) async-start(bf16[4,4,16,3,256]{4,2,1,3,0:T(8,128)(2,1)} %copy.30), calls=%async_computation.2 | async-start | bytes 786432 | tf_op jit(solution)/shard_map/all_to_all | solution.py:159
  59.1 11.2 %all-to-all-done.2 = bf16[4,4,16,3,256]{4,2,1,3,0:T(8,128)(2,1)S(1)} async-done(((bf16[4,4,16,3,256]{4,2,1,3,0:T(8,128)(2,1)}), bf16[4,4,16,3,256]{4,2,1,3,0:T(8,128)(2,1)S(1)}, u32[]{:S(2)}, u32[]{:S(2)}) %all-to-all-start.2) | async-done | bytes 393248 | tf_op jit(solution)/shard_map/all_to_all | solution.py:159
  70.3 0.8 copy.31
  71.1 3.5 %all-to-all-start.3 = ((bf16[4,4,16,3,256]{4,2,0,3,1:T(8,128)(2,1)}), bf16[4,4,16,3,256]{4,2,0,3,1:T(8,128)(2,1)S(1)}, u32[]{:S(2)}, u32[]{:S(2)}) async-start(bf16[4,4,16,3,256]{4,2,0,3,1:T(8,128)(2,1)} %copy.31), calls=%async_computation.3 | async-start | bytes 786432 | tf_op jit(solution)/shard_map/all_to_all | solution.py:158
  74.7 7.3 %all-to-all-done.3 = bf16[4,4,16,3,256]{4,2,0,3,1:T(8,128)(2,1)S(1)} async-done(((bf16[4,4,16,3,256]{4,2,0,3,1:T(8,128)(2,1)}), bf16[4,4,16,3,256]{4,2,0,3,1:T(8,128)(2,1)S(1)}, u32[]{:S(2)}, u32[]{:S(2)}) %all-to-all-start.3) | async-done | bytes 393248 | tf_op jit(solution)/shard_map/all_to_all | solution.py:158
  82.0 0.3 copy.33
  82.5 7.0 %scatter_fusion = bf16[256,3,256]{2,1,0:T(4,128)(2,1)S(1)} fusion(bf16[256,3,256]{2,1,0:T(4,128)(2,1)S(1)} %broadcast_in_dim.225, s32[256]{0:T(256)S(1)} %bitcast.261, bf16[256,3,256]{2,1,0:T(4,128)(2,1)S(1)} %copy.33), kind=kCustom, calls=%fused_computation.4 | custom fusion | bytes 1180672 | tf_op jit(solution)/shard_map/scatter | solution.py:176
  89.5 0.5 fusion.89
  90.1 1.2 copy-done.7
  91.3 0.5 fusion.20
  91.8 0.6 copy-done.6
  92.3 0.8 fusion.8
  93.2 0.8 fusion.37
  94.0 3.8 %stack.135 = f32[6]{0:T(128)S(1)} concatenate(f32[1]{0:T(128)} %bitcast.30, f32[1]{0:T(128)} %bitcast.32, f32[1]{0:T(128)} %bitcast.34, f32[1]{0:T(128)} %bitcast.36, f32[1]{0:T(128)} %bitcast.38, f32[1]{0:T(128)} %bitcast.39), dimensions={0} | concatenate | bytes 48 | tf_op jit(solution)/shard_map/stack | solution.py:106
  98.0 30.2 %all-reduce.16 = f32[96]{0:T(128)S(1)} all-reduce(f32[96]{0:T(128)S(1)} %dynamic-update-slice), channel_id=2, replica_groups=mesh['groups'=2,'patch'=4,'sub'=2,'half'=2] {'patch','sub','half'}, use_global_device_ids=true, to_apply=%add.16 | all-reduce | flops 96 | bytes 768
  128.3 0.7 fusion.91
  135.4 1.0 fusion.41
  136.9 0.9 copy-done.3
  138.0 12.3 %gather_fusion.3 = f32[1024]{0:T(1024)S(1)} fusion(f32[2,2,128,256]{3,2,1,0:T(8,128)S(1)} %get-tuple-element.46, s32[1024]{0:T(1024)S(1)} %bitcast.214), kind=kCustom, calls=%fused_computation.3.clone | custom fusion | bytes 24576 | tf_op jit(solution)/shard_map/jit(take_along_axis)/gather | solution.py:72
  150.3 12.3 %gather_fusion.2 = f32[1024]{0:T(1024)S(1)} fusion(f32[2,2,128,256]{3,2,1,0:T(8,128)S(1)} %get-tuple-element.46, s32[1024]{0:T(1024)S(1)} %bitcast.212), kind=kCustom, calls=%fused_computation.2.clone | custom fusion | bytes 24576 | tf_op jit(solution)/shard_map/jit(take_along_axis)/gather | solution.py:72
  162.9 3.8 %collective-permute-start.5 = (f32[2,2,2,2,256]{4,3,2,1,0:T(2,128)S(1)}, f32[2,2,2,2,256]{4,3,2,1,0:T(2,128)S(1)}, u32[]{:S(2)}, u32[]{:S(2)}) collective-permute-start(f32[2,2,2,2,256]{4,3,2,1,0:T(2,128)S(1)} %pad_maximum_fusion.5), channel_id=1, source_target_pairs={{0,12},{4,0},{8,4},{12,8},{1,13},{5,1},{9,5},{13,9},{2,14},{6,2},{... | collective-permute-start | bytes 49160 | tf_op jit(solution)/shard_map/ppermute | solution.py:15
  166.7 0.4 fusion.25
  167.4 1.1 collective-permute-done.4
  168.9 0.6 fusion.17
  169.5 0.3 copy-done.8
  170.0 0.8 fusion.33
  170.8 3.8 %stack.150 = f32[6]{0:T(128)S(1)} concatenate(f32[1]{0:T(128)} %bitcast.60, f32[1]{0:T(128)} %bitcast.62, f32[1]{0:T(128)} %bitcast.63, f32[1]{0:T(128)} %bitcast.65, f32[1]{0:T(128)} %bitcast.67, f32[1]{0:T(128)} %bitcast.68), dimensions={0} | concatenate | bytes 48 | tf_op jit(solution)/shard_map/stack | solution.py:106
  174.9 29.5 %all-reduce.17 = f32[96]{0:T(128)S(1)} all-reduce(f32[96]{0:T(128)S(1)} %dynamic-update-slice.1), channel_id=3, replica_groups=mesh['groups'=2,'patch'=4,'sub'=2,'half'=2] {'patch','sub','half'}, use_global_device_ids=true, to_apply=%add.17 | all-reduce | flops 96 | bytes 768
  204.4 0.7 fusion.90
  211.9 0.8 pad_maximum_fusion.1
  (117 shorter events, 4.8 us)
Async XLA Ops:
  0.0 0.7 copy-start.12
  27.1 31.7 %collective-permute-start.2 = (f32[2,2,2,2,256]{4,3,2,1,0:T(2,128)S(1)}, f32[2,2,2,2,256]{4,3,2,1,0:T(2,128)S(1)}, u32[]{:S(2)}, u32[]{:S(2)}) collective-permute-start(f32[2,2,2,2,256]{4,3,2,1,0:T(2,128)S(1)} %pad_maximum_fusion.4), channel_id=1, source_target_pairs={{0,4},{4,8},{8,12},{12,0},{1,5},{5,9},{9,13},{13,1},{2,6},{6,10},{... | collective-permute-start | bytes 49160 | tf_op jit(solution)/shard_map/ppermute | solution.py:15
  30.1 28.7 %collective-permute-start.3 = (f32[2,2,2,2,256]{4,3,2,1,0:T(2,128)S(1)}, f32[2,2,2,2,256]{4,3,2,1,0:T(2,128)S(1)}, u32[]{:S(2)}, u32[]{:S(2)}) collective-permute-start(f32[2,2,2,2,256]{4,3,2,1,0:T(2,128)S(1)} %pad_maximum_fusion.4), channel_id=1, source_target_pairs={{0,12},{4,0},{8,4},{12,8},{1,13},{5,1},{9,5},{13,9},{2,14},{6,2},{... | collective-permute-start | bytes 49160 | tf_op jit(solution)/shard_map/ppermute | solution.py:15
  32.2 0.7 copy-start.13
  32.9 3.9 %copy-start.11 = (s32[256]{0:T(256)S(1)}, s32[256]{0:T(256)}, u32[]{:S(2)}) copy-start(s32[256]{0:T(256)} %param.15) | copy-start | bytes 3076
  32.9 12.8 %collective-permute-start = (s32[2,2]{1,0:T(2,128)S(1)}, s32[2,2]{1,0:T(2,128)S(1)}, u32[]{:S(2)}, u32[]{:S(2)}) collective-permute-start(s32[2,2]{1,0:T(2,128)S(1)} %pad_add_fusion.4), channel_id=1, source_target_pairs={{0,4},{4,8},{8,12},{12,0},{1,5},{5,9},{9,13},{13,1},{2,6},{6,10},{... | collective-permute-start | bytes 56 | tf_op jit(solution)/shard_map/ppermute | solution.py:15
  33.0 12.8 %collective-permute-start.1 = (s32[2,2]{1,0:T(2,128)S(1)}, s32[2,2]{1,0:T(2,128)S(1)}, u32[]{:S(2)}, u32[]{:S(2)}) collective-permute-start(s32[2,2]{1,0:T(2,128)S(1)} %pad_add_fusion.4), channel_id=1, source_target_pairs={{0,12},{4,0},{8,4},{12,8},{1,13},{5,1},{9,5},{13,9},{2,14},{6,2},{... | collective-permute-start | bytes 56 | tf_op jit(solution)/shard_map/ppermute | solution.py:15
  37.5 8.8 %all-to-all-start = ((s32[4,4,16]{2,1,0:T(4,128)}), s32[4,4,16]{2,1,0:T(4,128)S(1)}, u32[]{:S(2)}, u32[]{:S(2)}) async-start(s32[4,4,16]{2,1,0:T(4,128)} %reshape.291), calls=%async_computation | async-start | bytes 16384 | tf_op jit(solution)/shard_map/all_to_all | solution.py:166
  40.8 1.1 copy-start
  41.8 1.0 copy-start.10
  42.8 1.0 copy-start.1
  43.8 0.7 copy-start.14
  46.9 7.0 %all-to-all-start.1 = ((s32[4,4,16]{2,0,1:T(4,128)}), s32[4,4,16]{2,0,1:T(4,128)S(1)}, u32[]{:S(2)}, u32[]{:S(2)}) async-start(s32[4,4,16]{2,0,1:T(4,128)} %copy.28), calls=%async_computation.1 | async-start | bytes 16384 | tf_op jit(solution)/shard_map/all_to_all | solution.py:165
  53.9 16.4 %all-to-all-start.2 = ((bf16[4,4,16,3,256]{4,2,1,3,0:T(8,128)(2,1)}), bf16[4,4,16,3,256]{4,2,1,3,0:T(8,128)(2,1)S(1)}, u32[]{:S(2)}, u32[]{:S(2)}) async-start(bf16[4,4,16,3,256]{4,2,1,3,0:T(8,128)(2,1)} %copy.30), calls=%async_computation.2 | async-start | bytes 786432 | tf_op jit(solution)/shard_map/all_to_all | solution.py:159
  71.1 10.9 %all-to-all-start.3 = ((bf16[4,4,16,3,256]{4,2,0,3,1:T(8,128)(2,1)}), bf16[4,4,16,3,256]{4,2,0,3,1:T(8,128)(2,1)S(1)}, u32[]{:S(2)}, u32[]{:S(2)}) async-start(bf16[4,4,16,3,256]{4,2,0,3,1:T(8,128)(2,1)} %copy.31), calls=%async_computation.3 | async-start | bytes 786432 | tf_op jit(solution)/shard_map/all_to_all | solution.py:158
  90.1 1.2 copy-start.7
  90.1 1.6 copy-start.2
  90.1 1.6 copy-start.4
  91.3 1.0 copy-start.6
  136.8 1.0 copy-start.3
  136.8 1.0 copy-start.5
  162.9 5.6 %collective-permute-start.4 = (f32[2,2,2,2,256]{4,3,2,1,0:T(2,128)S(1)}, f32[2,2,2,2,256]{4,3,2,1,0:T(2,128)S(1)}, u32[]{:S(2)}, u32[]{:S(2)}) collective-permute-start(f32[2,2,2,2,256]{4,3,2,1,0:T(2,128)S(1)} %pad_maximum_fusion.5), channel_id=1, source_target_pairs={{0,4},{4,8},{8,12},{12,0},{1,5},{5,9},{9,13},{13,1},{2,6},{6,10},{... | collective-permute-start | bytes 49160 | tf_op jit(solution)/shard_map/ppermute | solution.py:15
  162.9 5.5 %collective-permute-start.5 = (f32[2,2,2,2,256]{4,3,2,1,0:T(2,128)S(1)}, f32[2,2,2,2,256]{4,3,2,1,0:T(2,128)S(1)}, u32[]{:S(2)}, u32[]{:S(2)}) collective-permute-start(f32[2,2,2,2,256]{4,3,2,1,0:T(2,128)S(1)} %pad_maximum_fusion.5), channel_id=1, source_target_pairs={{0,12},{4,0},{8,4},{12,8},{1,13},{5,1},{9,5},{13,9},{2,14},{6,2},{... | collective-permute-start | bytes 49160 | tf_op jit(solution)/shard_map/ppermute | solution.py:15
  168.9 1.0 copy-start.8
  168.9 1.0 copy-start.9
